TPU v7x, 32 devices: a whole 2x2x4 slice. The times are simulated.
32 devices in a mesh: grp: 2 (over x), row: 8 (over z, y), col: 2 (over core).
Axes of the slice: x: 2, y: 2, z: 4, core: 2. Of those that a mesh axis runs over, the one named last changes fastest.
Arguments:
- query_window: bfloat16 [16, 8, 128, 1280], P(('grp', 'row'), 'col'), parts along dimension 0, may hold values from -80 to 80
- key_window: bfloat16 [16, 8, 128, 1280], P(('grp', 'row'), 'col'), parts along dimension 0, may hold values from -9 to 9
- value_window: bfloat16 [16, 8, 128, 1280], P(('grp', 'row'), 'col'), parts along dimension 0, may hold values from -6 to 6
- query_index: bfloat16 [16, 8, 128, 1280], P(('grp', 'row'), 'col'), parts along dimension 0, may hold values from -80 to 80
- key_index: bfloat16 [16, 8, 128, 1280], P(('grp', 'row'), 'col'), parts along dimension 0, may hold values from -9 to 9
- proj_weight: bfloat16 [1280, 1024], replicated, may hold values from -0.5 to 0.5
- proj_bias: float32 [1024], replicated, may hold values from -3 to 3
- first_kernel: bfloat16 [3, 3, 256, 256], replicated, may hold values from -0.125 to 0.125
- first_bias: float32 [256], replicated, may hold values from -3 to 3
- second_kernel: bfloat16 [3, 3, 256, 256], replicated, may hold values from -0.125 to 0.125
- second_bias: float32 [256], replicated, may hold values from -3 to 3
Outputs:
- fine_field: bfloat16 [256, 256, 256], P(('grp', 'row'), 'col'), parts along dimension 0
There are 2 independent parts, one for each index of `grp`. A program takes and returns all parts, laid end to end along the dimension named above; an argument that names none is the same for every part. Nothing has to cross between parts.
All inputs are finite; a program needn't handle non-finite values.
Results may differ from a plain program's by a relative error of at most 0.0048.
Values may be sent and summed in bfloat16 or wider, within the bound.
A program may use at most 64 MiB of HBM per device.

v0:
```python
import math
import jax
import jax.numpy as jnp
from jax import lax
from jax.sharding import PartitionSpec as P

HEADS = 8
HEAD_DIM = 160
CHANNELS = 256
TILE_ROWS = 8
TILE_COLS = 16


def extended(value, sides, width):
    for axis, dim in sides:
        size, length = (lax.axis_size(axis), value.shape[dim])
        up = [(i, (i + 1) % size) for i in range(size - 1)]
        down = [(j, i) for i, j in up]
        last = lax.slice_in_dim(value, length - width, length, axis=dim)
        first = lax.slice_in_dim(value, 0, width, axis=dim)
        before = lax.ppermute(last, axis, up)
        after = lax.ppermute(first, axis, down)
        value = jnp.concatenate([before, value, after], axis=dim)
    return value


def softmax_rows(scores):
    highest = jnp.max(scores, axis=-1, keepdims=True)
    raised = jnp.exp(scores - highest)
    return (raised / jnp.sum(raised, axis=-1, keepdims=True)).astype(jnp.bfloat16)


def window_attend(queries, key_rows, values):
    scores = jnp.einsum(
        "blhd,bmhd->bhlm", queries, key_rows, preferred_element_type=jnp.float32
    ) / math.sqrt(HEAD_DIM)
    weights = softmax_rows(scores)
    return jnp.einsum(
        "bhlm,bmhd->blhd", weights, values, preferred_element_type=jnp.float32
    ).astype(jnp.bfloat16)


def index_attend(queries, key_rows, values):
    scores = jnp.einsum(
        "lbhd,mbhd->bhlm", queries, key_rows, preferred_element_type=jnp.float32
    ) / math.sqrt(HEAD_DIM)
    weights = softmax_rows(scores)
    return jnp.einsum(
        "bhlm,mbhd->lbhd", weights, values, preferred_element_type=jnp.float32
    ).astype(jnp.bfloat16)


def convolve(image, kernel, bias):
    height, breadth, depth = image.shape
    padded = extended(image, (("row", 0), ("col", 1)), 1)
    total = jnp.zeros((height * breadth, kernel.shape[-1]), jnp.float32)
    for row_shift in range(3):
        for col_shift in range(3):
            cells = padded[row_shift : row_shift + height, col_shift : col_shift + breadth].reshape(
                -1, depth
            )
            total = total + jnp.dot(
                cells, kernel[row_shift, col_shift], preferred_element_type=jnp.float32
            )
    return (total + bias).reshape(height, breadth, -1)


def shards(
    query_window,
    key_window,
    value_window,
    query_index,
    key_index,
    proj_weight,
    proj_bias,
    first_kernel,
    first_bias,
    second_kernel,
    second_bias,
):
    rows_dev, cols_dev, tokens_win, features = query_window.shape
    layout = (rows_dev * cols_dev, tokens_win, HEADS, HEAD_DIM)
    window_out = window_attend(
        query_window.reshape(layout), key_window.reshape(layout), value_window.reshape(layout)
    ).reshape(query_window.shape)
    count_row = lax.axis_size("row")
    count_col = lax.axis_size("col")
    owned_tokens = tokens_win // (count_row * count_col)
    moved = (
        lax.all_to_all(query_index, ("row", "col"), split_axis=2, concat_axis=0, tiled=True),
        lax.all_to_all(key_index, ("row", "col"), split_axis=2, concat_axis=0, tiled=True),
        lax.all_to_all(window_out, ("row", "col"), split_axis=2, concat_axis=0, tiled=True),
    )
    owner_shape = moved[0].shape
    across = (-1, owned_tokens, HEADS, HEAD_DIM)
    index_out = index_attend(
        moved[0].reshape(across), moved[1].reshape(across), moved[2].reshape(across)
    )
    index_rows = index_out.reshape(-1, features)
    owner_rows = (
        jnp.dot(index_rows, proj_weight, preferred_element_type=jnp.float32) + proj_bias
    ).astype(jnp.bfloat16)
    last = owner_rows.shape[-1]
    shaped = owner_rows.reshape(tuple(owner_shape[:-1]) + (last,))
    returned = lax.all_to_all(shaped, ("row", "col"), split_axis=0, concat_axis=2, tiled=True)
    projected = returned.reshape(rows_dev * cols_dev * tokens_win, last)
    grouped = projected.reshape(rows_dev, cols_dev, TILE_ROWS, TILE_COLS, 2, 2, CHANNELS)
    shuffled = jnp.transpose(grouped, (0, 2, 4, 1, 3, 5, 6)).reshape(
        rows_dev * TILE_ROWS * 2, cols_dev * TILE_COLS * 2, CHANNELS
    )
    activated = jax.nn.gelu(convolve(shuffled, first_kernel, first_bias)).astype(jnp.bfloat16)
    return convolve(activated, second_kernel, second_bias).astype(jnp.bfloat16)


def solution(mesh):
    in_specs = (
        P(("grp", "row"), "col", None, None),
        P(("grp", "row"), "col", None, None),
        P(("grp", "row"), "col", None, None),
        P(("grp", "row"), "col", None, None),
        P(("grp", "row"), "col", None, None),
        P(),
        P(),
        P(),
        P(),
        P(),
        P(),
    )
    out_specs = P(("grp", "row"), "col", None)
    return jax.shard_map(shards, mesh=mesh, in_specs=in_specs, out_specs=out_specs, check_vma=False)
```

profile of v0, /device:TPU:9, one launch (start us, length us, event | category | flops | bytes accessed | tf_op | source)
XLA Modules:
  0.0 240.3 jit_solution(4875045535725694193)
XLA Ops:
  0.0 2.6 %copy.35 = bf16[1,4,128,1280]{2,3,1,0:T(8,128)(2,1)} copy(bf16[1,4,128,1280]{3,2,1,0:T(8,128)(2,1)} %param.13) | data formatting | bytes 2621440 | tf_op args[2]
  2.6 2.4 %copy.33 = bf16[1,4,128,1280]{2,3,1,0:T(8,128)(2,1)} copy(bf16[1,4,128,1280]{3,2,1,0:T(8,128)(2,1)} %param.11) | data formatting | bytes 2621440 | tf_op args[0]
  5.0 2.4 %copy.34 = bf16[1,4,128,1280]{2,3,1,0:T(8,128)(2,1)} copy(bf16[1,4,128,1280]{3,2,1,0:T(8,128)(2,1)} %param.12) | data formatting | bytes 2621440 | tf_op args[1]
  7.4 2.5 %fusion.114 = f32[4,8,128,128]{2,3,1,0:T(8,128)S(1)} fusion(bf16[4,128,8,160]{1,3,2,0:T(8,128)(2,1)} %bitcast.137, bf16[4,128,8,160]{1,3,2,0:T(8,128)(2,1)} %bitcast.138), kind=kOutput, calls=%fused_computation.150 | convolution fusion | flops 167772160 | bytes 4718592 | tf_op jit(solution)/shard_map/blhd,bmhd->bhlm/dot_general | solution.py:34
  9.9 1.3 copy-done.4
  11.2 0.5 fusion.112
  11.8 3.9 %convolution_convert_fusion = bf16[4,8,128,160]{2,3,1,0:T(8,128)(2,1)} fusion(bf16[4,128,8,160]{1,3,2,0:T(8,128)(2,1)} %bitcast.160, f32[4,8,128]{2,1,0:T(8,128)S(1)} %fusion.112, f32[4,8,128,128]{2,3,1,0:T(8,128)} %copy-done.4), kind=kOutput, calls=%fused_computation.58 | convolution fusion | flops 170528896 | bytes 4734976 | tf_op jit(solution)/shard_map/bhlm,bmhd->blhd/dot_general | solution.py:38
  15.7 3.7 %copy.37 = bf16[1,4,128,1280]{3,1,0,2:T(4,128)(2,1)} copy(bf16[1,4,128,1280]{2,3,1,0:T(8,128)(2,1)} %bitcast.161) | data formatting | bytes 2621440 | tf_op jit(solution)/shard_map/reshape | solution.py:85
  19.4 6.6 %all-to-all-start = ((bf16[1,4,128,1280]{3,1,0,2:T(4,128)(2,1)}), bf16[1,4,128,1280]{3,1,0,2:T(4,128)(2,1)}, u32[]{:S(2)}, u32[]{:S(2)}) async-start(bf16[1,4,128,1280]{3,1,0,2:T(4,128)(2,1)} %copy.37), calls=%async_computation | async-start | bytes 2621440 | tf_op jit(solution)/shard_map/all_to_all | solution.py:92
  26.0 3.4 %copy.42 = bf16[1,4,128,1280]{3,1,0,2:T(4,128)(2,1)} copy(bf16[1,4,128,1280]{3,2,1,0:T(8,128)(2,1)} %param.15) | data formatting | bytes 2621440 | tf_op args[4]
  29.4 27.0 %all-to-all-done = bf16[1,4,128,1280]{3,1,0,2:T(4,128)(2,1)} async-done(((bf16[1,4,128,1280]{3,1,0,2:T(4,128)(2,1)}), bf16[1,4,128,1280]{3,1,0,2:T(4,128)(2,1)}, u32[]{:S(2)}, u32[]{:S(2)}) %all-to-all-start) | async-done | bytes 1310752 | tf_op jit(solution)/shard_map/all_to_all | solution.py:92
  56.4 5.0 %all-to-all-start.2 = ((bf16[1,4,128,1280]{3,1,0,2:T(4,128)(2,1)}), bf16[1,4,128,1280]{3,1,0,2:T(4,128)(2,1)}, u32[]{:S(2)}, u32[]{:S(2)}) async-start(bf16[1,4,128,1280]{3,1,0,2:T(4,128)(2,1)} %copy.42), calls=%async_computation.2 | async-start | bytes 2621440 | tf_op jit(solution)/shard_map/all_to_all | solution.py:91
  61.4 3.4 %copy.40 = bf16[1,4,128,1280]{3,1,0,2:T(4,128)(2,1)} copy(bf16[1,4,128,1280]{3,2,1,0:T(8,128)(2,1)} %param.14) | data formatting | bytes 2621440 | tf_op args[3]
  64.8 27.0 %all-to-all-done.2 = bf16[1,4,128,1280]{3,1,0,2:T(4,128)(2,1)} async-done(((bf16[1,4,128,1280]{3,1,0,2:T(4,128)(2,1)}), bf16[1,4,128,1280]{3,1,0,2:T(4,128)(2,1)}, u32[]{:S(2)}, u32[]{:S(2)}) %all-to-all-start.2) | async-done | bytes 1310752 | tf_op jit(solution)/shard_map/all_to_all | solution.py:91
  91.8 5.0 %all-to-all-start.1 = ((bf16[1,4,128,1280]{3,1,0,2:T(4,128)(2,1)}), bf16[1,4,128,1280]{3,1,0,2:T(4,128)(2,1)}, u32[]{:S(2)}, u32[]{:S(2)}) async-start(bf16[1,4,128,1280]{3,1,0,2:T(4,128)(2,1)} %copy.40), calls=%async_computation.1 | async-start | bytes 2621440 | tf_op jit(solution)/shard_map/all_to_all | solution.py:90
  96.8 1.4 copy.67
  98.3 1.2 copy.39
  99.5 4.8 %reshape.99 = bf16[64,8,8,160]{3,2,1,0:T(8,128)(2,1)} reshape(bf16[16,1,4,8,1280]{4,3,2,0,1:T(8,128)(2,1)} %copy.39) | data formatting | bytes 2621440 | tf_op jit(solution)/shard_map/reshape | solution.py:97
  104.3 2.5 %copy.65 = bf16[1,4,16,8,1280]{4,3,1,2,0:T(8,128)(2,1)} copy(bf16[1,4,16,8,1280]{4,1,3,2,0:T(4,128)(2,1)} %bitcast.9) | data formatting | bytes 2621440 | tf_op jit(solution)/shard_map/all_to_all | solution.py:91
  106.9 4.8 %reshape.101 = bf16[64,8,8,160]{3,2,1,0:T(8,128)(2,1)} reshape(bf16[16,1,4,8,1280]{4,3,2,0,1:T(8,128)(2,1)} %bitcast.140) | data formatting | bytes 2621440 | tf_op jit(solution)/shard_map/reshape | solution.py:97
  111.7 15.5 %all-to-all-done.1 = bf16[1,4,128,1280]{3,1,0,2:T(4,128)(2,1)} async-done(((bf16[1,4,128,1280]{3,1,0,2:T(4,128)(2,1)}), bf16[1,4,128,1280]{3,1,0,2:T(4,128)(2,1)}, u32[]{:S(2)}, u32[]{:S(2)}) %all-to-all-start.1) | async-done | bytes 1310752 | tf_op jit(solution)/shard_map/all_to_all | solution.py:90
  127.2 2.5 %copy.66 = bf16[1,4,16,8,1280]{4,3,1,2,0:T(8,128)(2,1)} copy(bf16[1,4,16,8,1280]{4,1,3,2,0:T(4,128)(2,1)} %bitcast.7) | data formatting | bytes 2621440 | tf_op jit(solution)/shard_map/all_to_all | solution.py:90
  129.7 4.8 %reshape.100 = bf16[64,8,8,160]{3,2,1,0:T(8,128)(2,1)} reshape(bf16[16,1,4,8,1280]{4,3,2,0,1:T(8,128)(2,1)} %bitcast.141) | data formatting | bytes 2621440 | tf_op jit(solution)/shard_map/reshape | solution.py:97
  134.6 4.6 %fusion.26 = f32[8,8,64,64]{2,3,1,0:T(8,128)S(1)} fusion(bf16[64,8,8,160]{3,2,1,0:T(8,128)(2,1)} %reshape.101, bf16[64,8,8,160]{3,2,1,0:T(8,128)(2,1)} %reshape.100), kind=kOutput, calls=%fused_computation.41 | convolution fusion | flops 83886080 | bytes 3670016 | tf_op jit(solution)/shard_map/lbhd,mbhd->bhlm/dot_general | solution.py:44
  139.2 1.3 copy-done.3
  140.5 0.6 fusion.113
  141.2 5.6 %convert_bitcast_fusion = bf16[64,8,8,160]{3,0,2,1:T(8,128)(2,1)} fusion(bf16[64,8,8,160]{3,2,1,0:T(8,128)(2,1)} %reshape.99, f32[8,8,64]{2,1,0:T(8,128)S(1)} %fusion.113, f32[8,8,64,64]{2,3,1,0:T(8,128)} %copy-done.3), kind=kOutput, calls=%fused_computation.45 | convolution fusion | flops 85594176 | bytes 3686400 | tf_op jit(solution)/shard_map/bhlm,mbhd->lbhd/dot_general | solution.py:48
  146.8 4.1 %copy.48 = bf16[64,8,8,160]{3,2,1,0:T(8,128)(2,1)} copy(bf16[64,8,8,160]{3,0,2,1:T(8,128)(2,1)} %convert_bitcast_fusion) | data formatting | bytes 2621440 | tf_op jit(solution)/shard_map/convert_element_type | solution.py:50
  150.9 4.6 %reshape.102 = bf16[512,1280]{1,0:T(8,128)(2,1)} reshape(bf16[64,8,8,160]{3,2,1,0:T(8,128)(2,1)} %copy.48) | data formatting | bytes 2621440 | tf_op jit(solution)/shard_map/reshape | solution.py:99
  155.5 2.8 %add_convert_fusion = bf16[512,1024]{1,0:T(8,128)(2,1)S(1)} fusion(bf16[512,1280]{1,0:T(8,128)(2,1)} %reshape.102, bf16[1280,1024]{1,0:T(8,128)(2,1)S(1)} %copy-done, f32[1024]{0:T(1024)S(1)} %copy-done.9), kind=kOutput, calls=%fused_computation.44 | convolution fusion | flops 1343225856 | bytes 4984832 | tf_op jit(solution)/shard_map/dot_general | solution.py:101
  158.4 30.2 %all_to_all.60 = bf16[16,4,8,1024]{3,2,1,0:T(8,128)(2,1)S(1)} all-to-all(bf16[16,4,8,1024]{3,2,1,0:T(8,128)(2,1)S(1)} %bitcast.162), channel_id=1, replica_groups=mesh['grp'=2,'row'=8,'col'=2] {'row','col'}, dimensions={0} | all-to-all | bytes 2097152 | tf_op jit(solution)/shard_map/all_to_all | solution.py:105
  188.6 1.6 reshape_reshape.6
  190.2 2.4 copy.50
  192.6 0.4 reshape.104
  193.1 2.5 %collective-permute-start = (bf16[1,128,256]{2,1,0:T(8,128)(2,1)S(1)}, bf16[1,128,256]{2,1,0:T(8,128)(2,1)S(1)}, u32[]{:S(2)}, u32[]{:S(2)}) collective-permute-start(bf16[1,128,256]{2,1,0:T(8,128)(2,1)S(1)} %get-tuple-element.34), channel_id=1, source_target_pairs={{0,2},{2,4},{4,6},{6,8},{8,10},{10,12},{12,14},{1,3},{3,5},{5,7},{... | collective-permute-start | bytes 196616 | tf_op jit(solution)/shard_map/ppermute | solution.py:21
  195.6 1.2 reshape_reshape.7
  196.8 3.6 %collective-permute-start.1 = (bf16[1,128,256]{2,1,0:T(8,128)(2,1)S(1)}, bf16[1,128,256]{2,1,0:T(8,128)(2,1)S(1)}, u32[]{:S(2)}, u32[]{:S(2)}) collective-permute-start(bf16[1,128,256]{2,1,0:T(8,128)(2,1)S(1)} %get-tuple-element.33), channel_id=1, source_target_pairs={{2,0},{4,2},{6,4},{8,6},{10,8},{12,10},{14,12},{3,1},{5,3},{7,5},{... | collective-permute-start | bytes 196616 | tf_op jit(solution)/shard_map/ppermute | solution.py:22
  200.5 1.3 collective-permute-done.1
  202.2 1.3 collective-permute-start.2
  203.5 3.5 %collective-permute-start.3 = (bf16[18,1,256]{2,1,0:T(2,128)(2,1)S(1)}, bf16[18,1,256]{2,1,0:T(2,128)(2,1)S(1)}, u32[]{:S(2)}, u32[]{:S(2)}) collective-permute-start(bf16[18,1,256]{2,1,0:T(2,128)(2,1)S(1)} %get-tuple-element.25), channel_id=1, source_target_pairs={{1,0},{3,2},{5,4},{7,6},{9,8},{11,10},{13,12},{15,14},{17,16},{19,... | collective-permute-start | bytes 27656 | tf_op jit(solution)/shard_map/ppermute | solution.py:22
  207.8 3.7 %pad_maximum_fusion.5 = (bf16[16,128,256]{2,1,0:T(8,128)(2,1)S(1)}, bf16[16,128,256]{2,1,0:T(8,128)(2,1)S(1)}, bf16[16,128,256]{2,1,0:T(8,128)(2,1)S(1)}, bf16[1...) fusion(bf16[18,128,256]{2,1,0:T(8,128)(2,1)S(1)} %constant_dynamic-update-slice_, ...), kind=kLoop, calls=%fused_computation.76 | loop fusion | flops 12582912 | bytes 7489536 | tf_op jit(solution)/shard_map/concatenate | solution.py:23
  212.0 0.4 convolution_add_fusion.12
  212.4 0.4 convolution_add_fusion.11
  212.9 0.4 convolution_add_fusion.10
  213.3 0.8 copy-done.2
  214.5 0.4 convolution_add_fusion.8
  215.2 0.6 fusion.6
  215.8 0.7 fusion.15
  216.5 4.6 %collective-permute-start.5 = (bf16[1,128,256]{2,1,0:T(8,128)(2,1)S(1)}, bf16[1,128,256]{2,1,0:T(8,128)(2,1)S(1)}, u32[]{:S(2)}, u32[]{:S(2)}) collective-permute-start(bf16[1,128,256]{2,1,0:T(8,128)(2,1)S(1)} %get-tuple-element.29), channel_id=1, source_target_pairs={{2,0},{4,2},{6,4},{8,6},{10,8},{12,10},{14,12},{3,1},{5,3},{7,5},{... | collective-permute-start | bytes 196616 | tf_op jit(solution)/shard_map/ppermute | solution.py:22
  221.1 2.1 collective-permute-start.4
  223.3 3.9 %collective-permute-done.4 = bf16[1,128,256]{2,1,0:T(8,128)(2,1)S(1)} collective-permute-done((bf16[1,128,256]{2,1,0:T(8,128)(2,1)S(1)}, bf16[1,128,256]{2,1,0:T(8,128)(2,1)S(1)}, u32[]{:S(2)}, u32[]{:S(2)}) %collective-permute-start.4) | collective-permute-done | bytes 65568 | tf_op jit(solution)/shard_map/ppermute | solution.py:21
  227.2 1.3 collective-permute-start.6
  228.5 3.9 %collective-permute-start.7 = (bf16[18,1,256]{2,1,0:T(2,128)(2,1)S(1)}, bf16[18,1,256]{2,1,0:T(2,128)(2,1)S(1)}, u32[]{:S(2)}, u32[]{:S(2)}) collective-permute-start(bf16[18,1,256]{2,1,0:T(2,128)(2,1)S(1)} %get-tuple-element.20), channel_id=1, source_target_pairs={{1,0},{3,2},{5,4},{7,6},{9,8},{11,10},{13,12},{15,14},{17,16},{19,... | collective-permute-start | bytes 27656 | tf_op jit(solution)/shard_map/ppermute | solution.py:22
  232.6 0.4 fusion.54
  233.0 0.8 maximum_maximum_fusion
  233.9 1.0 fusion.107
  234.8 0.4 fusion.46
  235.3 0.4 convolution_add_fusion.6
  235.7 0.4 convolution_add_fusion.5
  236.2 0.5 convolution_add_fusion.4
  236.6 0.9 convolution_add_fusion.3
  237.5 0.5 convolution_add_fusion.2
  238.0 0.4 convolution_add_fusion.1
  238.6 1.5 fusion.7
  (36 shorter events, 3.2 us)
Async XLA Ops:
  0.0 155.5 %copy-start = (bf16[1280,1024]{1,0:T(8,128)(2,1)S(1)}, bf16[1280,1024]{1,0:T(8,128)(2,1)}, u32[]{:S(2)}) copy-start(bf16[1280,1024]{1,0:T(8,128)(2,1)} %param.16) | copy-start | bytes 7864324
  9.9 1.3 copy-start.4
  19.4 37.0 %all-to-all-start = ((bf16[1,4,128,1280]{3,1,0,2:T(4,128)(2,1)}), bf16[1,4,128,1280]{3,1,0,2:T(4,128)(2,1)}, u32[]{:S(2)}, u32[]{:S(2)}) async-start(bf16[1,4,128,1280]{3,1,0,2:T(4,128)(2,1)} %copy.37), calls=%async_computation | async-start | bytes 2621440 | tf_op jit(solution)/shard_map/all_to_all | solution.py:92
  56.4 35.4 %all-to-all-start.2 = ((bf16[1,4,128,1280]{3,1,0,2:T(4,128)(2,1)}), bf16[1,4,128,1280]{3,1,0,2:T(4,128)(2,1)}, u32[]{:S(2)}, u32[]{:S(2)}) async-start(bf16[1,4,128,1280]{3,1,0,2:T(4,128)(2,1)} %copy.42), calls=%async_computation.2 | async-start | bytes 2621440 | tf_op jit(solution)/shard_map/all_to_all | solution.py:91
  91.8 35.4 %all-to-all-start.1 = ((bf16[1,4,128,1280]{3,1,0,2:T(4,128)(2,1)}), bf16[1,4,128,1280]{3,1,0,2:T(4,128)(2,1)}, u32[]{:S(2)}, u32[]{:S(2)}) async-start(bf16[1,4,128,1280]{3,1,0,2:T(4,128)(2,1)} %copy.40), calls=%async_computation.1 | async-start | bytes 2621440 | tf_op jit(solution)/shard_map/all_to_all | solution.py:90
  139.2 1.3 copy-start.3
  150.9 4.6 %copy-start.9 = (f32[1024]{0:T(1024)S(1)}, f32[1024]{0:T(1024)}, u32[]{:S(2)}) copy-start(f32[1024]{0:T(1024)} %param.17) | copy-start | bytes 12292
  193.1 7.4 %collective-permute-start = (bf16[1,128,256]{2,1,0:T(8,128)(2,1)S(1)}, bf16[1,128,256]{2,1,0:T(8,128)(2,1)S(1)}, u32[]{:S(2)}, u32[]{:S(2)}) collective-permute-start(bf16[1,128,256]{2,1,0:T(8,128)(2,1)S(1)} %get-tuple-element.34), channel_id=1, source_target_pairs={{0,2},{2,4},{4,6},{6,8},{8,10},{10,12},{12,14},{1,3},{3,5},{5,7},{... | collective-permute-start | bytes 196616 | tf_op jit(solution)/shard_map/ppermute | solution.py:21
  196.8 5.0 %collective-permute-start.1 = (bf16[1,128,256]{2,1,0:T(8,128)(2,1)S(1)}, bf16[1,128,256]{2,1,0:T(8,128)(2,1)S(1)}, u32[]{:S(2)}, u32[]{:S(2)}) collective-permute-start(bf16[1,128,256]{2,1,0:T(8,128)(2,1)S(1)} %get-tuple-element.33), channel_id=1, source_target_pairs={{2,0},{4,2},{6,4},{8,6},{10,8},{12,10},{14,12},{3,1},{5,3},{7,5},{... | collective-permute-start | bytes 196616 | tf_op jit(solution)/shard_map/ppermute | solution.py:22
  200.5 6.5 %copy-start.5 = (bf16[3,3,256,256]{3,2,1,0:T(8,128)(2,1)S(1)}, bf16[3,3,256,256]{3,2,1,0:T(8,128)(2,1)}, u32[]{:S(2)}) copy-start(bf16[3,3,256,256]{3,2,1,0:T(8,128)(2,1)} %param.18) | copy-start | bytes 3538948
  202.2 5.6 %collective-permute-start.2 = (bf16[18,1,256]{2,1,0:T(2,128)(2,1)S(1)}, bf16[18,1,256]{2,1,0:T(2,128)(2,1)S(1)}, u32[]{:S(2)}, u32[]{:S(2)}) collective-permute-start(bf16[18,1,256]{2,1,0:T(2,128)(2,1)S(1)} %get-tuple-element.24), channel_id=1, source_target_pairs={{0,1},{2,3},{4,5},{6,7},{8,9},{10,11},{12,13},{14,15},{16,17},{18,... | collective-permute-start | bytes 27656 | tf_op jit(solution)/shard_map/ppermute | solution.py:21
  203.5 4.4 %collective-permute-start.3 = (bf16[18,1,256]{2,1,0:T(2,128)(2,1)S(1)}, bf16[18,1,256]{2,1,0:T(2,128)(2,1)S(1)}, u32[]{:S(2)}, u32[]{:S(2)}) collective-permute-start(bf16[18,1,256]{2,1,0:T(2,128)(2,1)S(1)} %get-tuple-element.25), channel_id=1, source_target_pairs={{1,0},{3,2},{5,4},{7,6},{9,8},{11,10},{13,12},{15,14},{17,16},{19,... | collective-permute-start | bytes 27656 | tf_op jit(solution)/shard_map/ppermute | solution.py:22
  212.8 1.2 copy-start.2
  214.5 0.7 copy-start.7
  216.5 6.8 %collective-permute-start.5 = (bf16[1,128,256]{2,1,0:T(8,128)(2,1)S(1)}, bf16[1,128,256]{2,1,0:T(8,128)(2,1)S(1)}, u32[]{:S(2)}, u32[]{:S(2)}) collective-permute-start(bf16[1,128,256]{2,1,0:T(8,128)(2,1)S(1)} %get-tuple-element.29), channel_id=1, source_target_pairs={{2,0},{4,2},{6,4},{8,6},{10,8},{12,10},{14,12},{3,1},{5,3},{7,5},{... | collective-permute-start | bytes 196616 | tf_op jit(solution)/shard_map/ppermute | solution.py:22
  221.1 11.4 %copy-start.6 = (bf16[3,3,256,256]{3,2,1,0:T(8,128)(2,1)S(1)}, bf16[3,3,256,256]{3,2,1,0:T(8,128)(2,1)}, u32[]{:S(2)}) copy-start(bf16[3,3,256,256]{3,2,1,0:T(8,128)(2,1)} %param.20) | copy-start | bytes 3538948
  221.1 6.0 %collective-permute-start.4 = (bf16[1,128,256]{2,1,0:T(8,128)(2,1)S(1)}, bf16[1,128,256]{2,1,0:T(8,128)(2,1)S(1)}, u32[]{:S(2)}, u32[]{:S(2)}) collective-permute-start(bf16[1,128,256]{2,1,0:T(8,128)(2,1)S(1)} %get-tuple-element.28), channel_id=1, source_target_pairs={{0,2},{2,4},{4,6},{6,8},{8,10},{10,12},{12,14},{1,3},{3,5},{5,7},{... | collective-permute-start | bytes 196616 | tf_op jit(solution)/shard_map/ppermute | solution.py:21
  227.2 5.8 %collective-permute-start.6 = (bf16[18,1,256]{2,1,0:T(2,128)(2,1)S(1)}, bf16[18,1,256]{2,1,0:T(2,128)(2,1)S(1)}, u32[]{:S(2)}, u32[]{:S(2)}) collective-permute-start(bf16[18,1,256]{2,1,0:T(2,128)(2,1)S(1)} %get-tuple-element.19), channel_id=1, source_target_pairs={{0,1},{2,3},{4,5},{6,7},{8,9},{10,11},{12,13},{14,15},{16,17},{18,... | collective-permute-start | bytes 27656 | tf_op jit(solution)/shard_map/ppermute | solution.py:21
  228.5 4.5 %collective-permute-start.7 = (bf16[18,1,256]{2,1,0:T(2,128)(2,1)S(1)}, bf16[18,1,256]{2,1,0:T(2,128)(2,1)S(1)}, u32[]{:S(2)}, u32[]{:S(2)}) collective-permute-start(bf16[18,1,256]{2,1,0:T(2,128)(2,1)S(1)} %get-tuple-element.20), channel_id=1, source_target_pairs={{1,0},{3,2},{5,4},{7,6},{9,8},{11,10},{13,12},{15,14},{17,16},{19,... | collective-permute-start | bytes 27656 | tf_op jit(solution)/shard_map/ppermute | solution.py:22
  238.0 0.7 copy-start.8
  238.4 1.9 copy-start.1
where the time goes:
time: 242 us; the launch traced here: 240 us
  waiting for transfers between devices  74.8 us (31%)
  local copies, waits for them, and re-layouts  59.8 us (25%)
  starting transfers between devices  39.4 us (16%)
  blocking collectives  30.2 us (12%)
  matrix products  29 us (12%)
  other arithmetic  6.82 us (3%)
    all_to_all x1, blocking collectives, shards(): lax.all_to_all(shaped, ('row', 'col'), split_axis=0, concat_axis=2, tiled...  30.2 us
    all_to_all x1, waiting for transfers between devices, shards(): lax.all_to_all(key_index, ('row', 'col'), split_axis=2, concat_axis=0, ti...  27 us
    all_to_all x1, waiting for transfers between devices, shards(): lax.all_to_all(window_out, ('row', 'col'), split_axis=2, concat_axis=0, t...  27 us
    unnamed x26, local copies, waits for them, and re-layouts  18.4 us
    ppermute x4, starting transfers between devices, extended(): after = lax.ppermute(first, axis, down)  15.6 us
    all_to_all x1, waiting for transfers between devices, shards(): lax.all_to_all(query_index, ('row', 'col'), split_axis=2, concat_axis=0,...  15.5 us
    dot_general x18, matrix products, convolve(): jnp.dot(cells, kernel[row_shift, col_shift], preferred_element_type=jnp.f...  9.53 us
    ppermute x4, starting transfers between devices, extended(): before = lax.ppermute(last, axis, up)  7.18 us
  transfers between devices with their start and end apart: 11, of which 6 were waited for; matrix products, arithmetic and copies ran while one was open for 10% of the time, Pallas kernels for 0%

commit v1 on v0

--- a/solution.py
+++ b/solution.py
@@ -9,6 +9,29 @@
 CHANNELS = 256
 TILE_ROWS = 8
 TILE_COLS = 16
+
+
+def in_blocks(x, dim, size):
+    before, after = (x.shape[:dim], x.shape[dim + 1 :])
+    return jnp.moveaxis(x.reshape(*before, size, -1, *after), dim, 0)
+
+
+def in_order(blocks, dim):
+    blocks = jnp.moveaxis(blocks, 0, dim)
+    shape = blocks.shape
+    return blocks.reshape(*shape[:dim], shape[dim] * shape[dim + 1], *shape[dim + 2 :])
+
+
+def exchange_directly(x, axis, split_dim, concat_dim):
+    length, index = (lax.axis_size(axis), lax.axis_index(axis))
+    tiles = in_blocks(x, split_dim, length)
+    out = tiles
+    for turn in range(1, length):
+        target, source = ((index + turn) % length, (index - turn) % length)
+        sent = lax.dynamic_index_in_dim(tiles, target, 0)
+        theirs = lax.ppermute(sent, axis, [(i, (i + turn) % length) for i in range(length)])
+        out = lax.dynamic_update_slice_in_dim(out, theirs, source, axis=0)
+    return in_order(out, concat_dim)
 
 
 def extended(value, sides, width):
@@ -89,7 +112,7 @@
     moved = (
         lax.all_to_all(query_index, ("row", "col"), split_axis=2, concat_axis=0, tiled=True),
         lax.all_to_all(key_index, ("row", "col"), split_axis=2, concat_axis=0, tiled=True),
-        lax.all_to_all(window_out, ("row", "col"), split_axis=2, concat_axis=0, tiled=True),
+        exchange_directly(window_out, ("row", "col"), 2, 0),
     )
     owner_shape = moved[0].shape
     across = (-1, owned_tokens, HEADS, HEAD_DIM)

time: 242 us -> 237 us (0.979)
  waiting for transfers between devices: 74.8 us -> 26.8 us
  local copies, waits for them, and re-layouts: 59.8 us -> 84.8 us
  starting transfers between devices: 39.4 us -> 54.4 us
  blocking collectives: 30.2 us -> 33.4 us
    all_to_all x1, waiting for transfers between devices: 27 us -> 0.01 us  [shards(): lax.all_to_all(key_index, ('row', 'col'), split_axis=2, concat_axis=0, ti...]
    all_to_all x1 -> x0, waiting for transfers between devices: 27 us -> none  [shards(): lax.all_to_all(window_out, ('row', 'col'), split_axis=2, concat_axis=0, t...]
    ppermute x0 -> x15, waiting for transfers between devices: none -> 21.5 us  [exchange_directly(): lax.ppermute(sent, axis, [(i, (i + turn) % length) for i in range(length)])]
    ppermute x0 -> x15, starting transfers between devices: none -> 20.9 us  [exchange_directly(): lax.ppermute(sent, axis, [(i, (i + turn) % length) for i in range(length)])]
    dynamic_update_slice x0 -> x16, local copies, waits for them, and re-layouts: none -> 20.3 us  [exchange_directly(): out = lax.dynamic_update_slice_in_dim(out, theirs, source, axis=0)]
    all_to_all x1, waiting for transfers between devices: 15.5 us -> 0.01 us  [shards(): lax.all_to_all(query_index, ('row', 'col'), split_axis=2, concat_axis=0,...]
    another operation x0 -> x2, local copies, waits for them, and re-layouts: none -> 9.41 us  [the longest x1 4.84 us: shards(): moved[2].reshape(across)]
    reshape x2 -> x0, local copies, waits for them, and re-layouts: 8.54 us -> none  [the longest x1 4.85 us: shards(): moved[2].reshape(across)]
  transfers between devices with their start and end apart: 11 -> 25, of which waited for: 6 -> 6; matrix products, arithmetic and copies ran while one was open for 10% -> 27% of each run, Pallas kernels for 0% -> 0%
where the time goes in v1:
time: 237 us; the launch traced here: 236 us
  local copies, waits for them, and re-layouts  84.8 us (36%)
  starting transfers between devices  54.4 us (23%)
  blocking collectives  33.4 us (14%)
  matrix products  29.1 us (12%)
  waiting for transfers between devices  26.8 us (11%)
  other arithmetic  6.82 us (3%)
    all_to_all x1, blocking collectives, shards(): lax.all_to_all(shaped, ('row', 'col'), split_axis=0, concat_axis=2, tiled...  33.4 us
    ppermute x15, waiting for transfers between devices, exchange_directly(): lax.ppermute(sent, axis, [(i, (i + turn) % length) for i in range(length)])  21.5 us
    ppermute x15, starting transfers between devices, exchange_directly(): lax.ppermute(sent, axis, [(i, (i + turn) % length) for i in range(length)])  20.9 us
    dynamic_update_slice x16, local copies, waits for them, and re-layouts, exchange_directly(): out = lax.dynamic_update_slice_in_dim(out, theirs, source, axis=0)  20.3 us
    unnamed x26, local copies, waits for them, and re-layouts  18.3 us
    ppermute x4, starting transfers between devices, extended(): after = lax.ppermute(first, axis, down)  15.5 us
    dot_general x18, matrix products, convolve(): jnp.dot(cells, kernel[row_shift, col_shift], preferred_element_type=jnp.f...  9.57 us
    ppermute x4, starting transfers between devices, extended(): before = lax.ppermute(last, axis, up)  7.18 us
  transfers between devices with their start and end apart: 25, of which 6 were waited for; matrix products, arithmetic and copies ran while one was open for 27% of the time, Pallas kernels for 0%

profile of v1, /device:TPU:9, one launch (start us, length us, event | category | flops | bytes accessed | tf_op | source)
XLA Modules:
  0.0 235.8 jit_solution(16063494384297852893)
XLA Ops:
  0.0 3.6 %copy.41 = bf16[1,4,128,1280]{3,1,0,2:T(4,128)(2,1)} copy(bf16[1,4,128,1280]{3,2,1,0:T(8,128)(2,1)} %param.15) | data formatting | bytes 2621440 | tf_op args[4]
  3.6 6.6 %all-to-all-start.1 = ((bf16[1,4,128,1280]{3,1,0,2:T(4,128)(2,1)}), bf16[1,4,128,1280]{3,1,0,2:T(4,128)(2,1)}, u32[]{:S(2)}, u32[]{:S(2)}) async-start(bf16[1,4,128,1280]{3,1,0,2:T(4,128)(2,1)} %copy.41), calls=%async_computation.1 | async-start | bytes 2621440 | tf_op jit(solution)/shard_map/all_to_all | solution.py:114
  10.1 2.4 %copy.35 = bf16[1,4,128,1280]{2,3,1,0:T(8,128)(2,1)} copy(bf16[1,4,128,1280]{3,2,1,0:T(8,128)(2,1)} %param.13) | data formatting | bytes 2621440 | tf_op args[2]
  12.6 2.4 %copy.33 = bf16[1,4,128,1280]{2,3,1,0:T(8,128)(2,1)} copy(bf16[1,4,128,1280]{3,2,1,0:T(8,128)(2,1)} %param.11) | data formatting | bytes 2621440 | tf_op args[0]
  15.0 2.4 %copy.34 = bf16[1,4,128,1280]{2,3,1,0:T(8,128)(2,1)} copy(bf16[1,4,128,1280]{3,2,1,0:T(8,128)(2,1)} %param.12) | data formatting | bytes 2621440 | tf_op args[1]
  17.4 2.5 %fusion.115 = f32[4,8,128,128]{2,3,1,0:T(8,128)S(1)} fusion(bf16[4,128,8,160]{1,3,2,0:T(8,128)(2,1)} %bitcast.165, bf16[4,128,8,160]{1,3,2,0:T(8,128)(2,1)} %bitcast.166), kind=kOutput, calls=%fused_computation.180 | convolution fusion | flops 167772160 | bytes 4718592 | tf_op jit(solution)/shard_map/blhd,bmhd->bhlm/dot_general | solution.py:57
  19.9 1.3 copy-done.4
  21.8 3.9 %fusion.33 = bf16[4,128,8,160]{1,3,2,0:T(8,128)(2,1)} fusion(bf16[4,128,8,160]{1,3,2,0:T(8,128)(2,1)} %bitcast.187, f32[4,8,128]{2,1,0:T(8,128)S(1)} %fusion.113, f32[4,8,128,128]{2,3,1,0:T(8,128)} %copy-done.4), kind=kOutput, calls=%fused_computation.59 | convolution fusion | flops 170528896 | bytes 4734976 | tf_op jit(solution)/shard_map/bhlm,bmhd->blhd/dot_general | solution.py:61
  25.7 4.3 %copy.37 = bf16[4,128,8,160]{3,2,1,0:T(8,128)(2,1)} copy(bf16[4,128,8,160]{1,3,2,0:T(8,128)(2,1)} %fusion.33) | data formatting | bytes 2621440 | tf_op jit(solution)/shard_map/convert_element_type | solution.py:63
  30.0 4.6 %reshape_reshape.12 = bf16[1,4,16,8,1280]{4,3,2,1,0:T(8,128)(2,1)} reshape(bf16[4,128,8,160]{3,2,1,0:T(8,128)(2,1)} %copy.37) | data formatting | bytes 2621440 | tf_op jit(solution)/shard_map/reshape;reshape | solution.py:16
  34.6 2.1 dynamic-slice_bitcast_fusion
  36.8 1.5 collective-permute-start
  38.2 1.2 collective-permute-start.1
  39.8 1.2 collective-permute-start.3
  41.0 2.5 %collective-permute-start.4 = (bf16[1,1,4,8,1280]{4,3,0,2,1:T(8,128)(2,1)S(1)}, bf16[1,1,4,8,1280]{4,3,0,2,1:T(8,128)(2,1)}, u32[]{:S(2)}, u32[]{:S(2)}) collective-permute-start(bf16[1,1,4,8,1280]{4,3,0,2,1:T(8,128)(2,1)S(1)} %get-tuple-element.15), channel_id=1, source_target_pairs={{0,5},{1,6},{2,7},{3,8},{4,9},{5,10},{6,11},{7,12},{8,13},{9,14},{... | collective-permute-start | bytes 245768 | tf_op jit(solution)/shard_map/ppermute | solution.py:32
  43.5 3.4 %copy.39 = bf16[1,4,128,1280]{3,1,0,2:T(4,128)(2,1)} copy(bf16[1,4,128,1280]{3,2,1,0:T(8,128)(2,1)} %param.14) | data formatting | bytes 2621440 | tf_op args[3]
  46.9 1.2 collective-permute-start.5
  48.1 1.5 constant_dynamic-update-slice_fusion.17
  49.6 1.2 collective-permute-start.6
  50.8 1.5 constant_dynamic-update-slice_fusion.16
  53.3 1.5 constant_dynamic-update-slice_fusion.15
  54.8 3.8 %collective-permute-start.8 = (bf16[1,1,4,8,1280]{4,3,0,2,1:T(8,128)(2,1)S(1)}, bf16[1,1,4,8,1280]{4,3,0,2,1:T(8,128)(2,1)}, u32[]{:S(2)}, u32[]{:S(2)}) collective-permute-start(bf16[1,1,4,8,1280]{4,3,0,2,1:T(8,128)(2,1)S(1)} %get-tuple-element.11), channel_id=1, source_target_pairs={{0,9},{1,10},{2,11},{3,12},{4,13},{5,14},{6,15},{7,0},{8,1},{9,2},... | collective-permute-start | bytes 245768 | tf_op jit(solution)/shard_map/ppermute | solution.py:32
  58.6 1.5 constant_dynamic-update-slice_fusion.14
  60.2 1.2 collective-permute-start.9
  61.3 4.3 %all-to-all-start = ((bf16[1,4,128,1280]{3,1,0,2:T(4,128)(2,1)}), bf16[1,4,128,1280]{3,1,0,2:T(4,128)(2,1)}, u32[]{:S(2)}, u32[]{:S(2)}) async-start(bf16[1,4,128,1280]{3,1,0,2:T(4,128)(2,1)} %copy.39), calls=%async_computation | async-start | bytes 2621440 | tf_op jit(solution)/shard_map/all_to_all | solution.py:113
  65.6 1.5 constant_dynamic-update-slice_fusion.13
  67.2 1.5 constant_dynamic-update-slice_fusion.12
  68.7 3.2 %collective-permute-start.11 = (bf16[1,1,4,8,1280]{4,3,0,2,1:T(8,128)(2,1)S(1)}, bf16[1,1,4,8,1280]{4,3,0,2,1:T(8,128)(2,1)S(1)}, u32[]{:S(2)}, u32[]{:S(2)}) collective-permute-start(bf16[1,1,4,8,1280]{4,3,0,2,1:T(8,128)(2,1)S(1)} %get-tuple-element.8), channel_id=1, source_target_pairs={{0,12},{1,13},{2,14},{3,15},{4,0},{5,1},{6,2},{7,3},{8,4},{9,5},{1... | collective-permute-start | bytes 245768 | tf_op jit(solution)/shard_map/ppermute | solution.py:32
  71.9 1.5 constant_dynamic-update-slice_fusion.11
  73.4 1.5 collective-permute-start.12
  74.9 1.5 constant_dynamic-update-slice_fusion.10
  76.4 1.2 collective-permute-start.13
  77.6 1.5 constant_dynamic-update-slice_fusion.9
  79.8 19.3 %collective-permute-done.10 = bf16[1,1,4,8,1280]{4,3,0,2,1:T(8,128)(2,1)S(1)} collective-permute-done((bf16[1,1,4,8,1280]{4,3,0,2,1:T(8,128)(2,1)S(1)}, bf16[1,1,4,8,1280]{4,3,0,2,1:T(8,128)(2,1)S(1)}, u32[]{:S(2)}, u32[]{:S(2)}) %collective-permute-start.10) | collective-permute-done | bytes 81952 | tf_op jit(solution)/shard_map/ppermute | solution.py:32
  100.6 2.0 collective-permute-done.12
  104.5 2.6 %copy.38 = bf16[16,1,4,8,1280]{4,3,2,0,1:T(8,128)(2,1)} copy(bf16[16,1,4,8,1280]{4,3,0,2,1:T(8,128)(2,1)} %constant_dynamic-update-slice_fusion.3) | data formatting | bytes 2621440 | tf_op jit(solution)/shard_map/dynamic_update_slice | solution.py:33
  107.1 4.8 %reshape_reshape.13 = bf16[64,8,8,160]{3,2,1,0:T(8,128)(2,1)} reshape(bf16[16,1,4,8,1280]{4,3,2,0,1:T(8,128)(2,1)} %copy.38) | data formatting | bytes 2621440 | tf_op jit(solution)/shard_map/reshape;reshape | solution.py:120
  111.9 2.6 %copy.63 = bf16[1,4,16,8,1280]{4,3,1,2,0:T(8,128)(2,1)} copy(bf16[1,4,16,8,1280]{4,1,3,2,0:T(4,128)(2,1)} %bitcast.22) | data formatting | bytes 2621440 | tf_op jit(solution)/shard_map/all_to_all | solution.py:114
  114.5 4.8 %reshape.107 = bf16[64,8,8,160]{3,2,1,0:T(8,128)(2,1)} reshape(bf16[16,1,4,8,1280]{4,3,2,0,1:T(8,128)(2,1)} %bitcast.167) | data formatting | bytes 2621440 | tf_op jit(solution)/shard_map/reshape | solution.py:120
  119.4 2.6 %copy.64 = bf16[1,4,16,8,1280]{4,3,1,2,0:T(8,128)(2,1)} copy(bf16[1,4,16,8,1280]{4,1,3,2,0:T(4,128)(2,1)} %bitcast.20) | data formatting | bytes 2621440 | tf_op jit(solution)/shard_map/all_to_all | solution.py:113
  122.0 4.8 %reshape.106 = bf16[64,8,8,160]{3,2,1,0:T(8,128)(2,1)} reshape(bf16[16,1,4,8,1280]{4,3,2,0,1:T(8,128)(2,1)} %bitcast.168) | data formatting | bytes 2621440 | tf_op jit(solution)/shard_map/reshape | solution.py:120
  126.9 4.6 %fusion.26 = f32[8,8,64,64]{2,3,1,0:T(8,128)S(1)} fusion(bf16[64,8,8,160]{3,2,1,0:T(8,128)(2,1)} %reshape.107, bf16[64,8,8,160]{3,2,1,0:T(8,128)(2,1)} %reshape.106), kind=kOutput, calls=%fused_computation.41 | convolution fusion | flops 83886080 | bytes 3670016 | tf_op jit(solution)/shard_map/lbhd,mbhd->bhlm/dot_general | solution.py:67
  131.5 1.3 copy-done.3
  133.4 5.7 %convert_bitcast_fusion = bf16[64,8,8,160]{3,0,2,1:T(8,128)(2,1)} fusion(bf16[64,8,8,160]{3,2,1,0:T(8,128)(2,1)} %reshape_reshape.13, f32[8,8,64]{2,1,0:T(8,128)S(1)} %fusion.114, f32[8,8,64,64]{2,3,1,0:T(8,128)} %copy-done.3), kind=kOutput, calls=%fused_computation.45 | convolution fusion | flops 85594176 | bytes 3686400 | tf_op jit(solution)/shard_map/bhlm,mbhd->lbhd/dot_general | solution.py:71
  139.1 4.1 %copy.47 = bf16[64,8,8,160]{3,2,1,0:T(8,128)(2,1)} copy(bf16[64,8,8,160]{3,0,2,1:T(8,128)(2,1)} %convert_bitcast_fusion) | data formatting | bytes 2621440 | tf_op jit(solution)/shard_map/convert_element_type | solution.py:73
  143.1 4.6 %reshape.108 = bf16[512,1280]{1,0:T(8,128)(2,1)} reshape(bf16[64,8,8,160]{3,2,1,0:T(8,128)(2,1)} %copy.47) | data formatting | bytes 2621440 | tf_op jit(solution)/shard_map/reshape | solution.py:122
  147.7 2.8 %add_convert_fusion = bf16[512,1024]{1,0:T(8,128)(2,1)S(1)} fusion(bf16[512,1280]{1,0:T(8,128)(2,1)} %reshape.108, bf16[1280,1024]{1,0:T(8,128)(2,1)S(1)} %copy-done, f32[1024]{0:T(1024)S(1)} %copy-done.9), kind=kOutput, calls=%fused_computation.44 | convolution fusion | flops 1343225856 | bytes 4984832 | tf_op jit(solution)/shard_map/dot_general | solution.py:124
  150.6 33.4 %all_to_all.45 = bf16[16,4,8,1024]{3,2,1,0:T(8,128)(2,1)S(1)} all-to-all(bf16[16,4,8,1024]{3,2,1,0:T(8,128)(2,1)S(1)} %bitcast.188), channel_id=1, replica_groups=mesh['grp'=2,'row'=8,'col'=2] {'row','col'}, dimensions={0} | all-to-all | bytes 2097152 | tf_op jit(solution)/shard_map/all_to_all | solution.py:128
  184.1 1.6 reshape_reshape.14
  185.7 2.4 %copy.49 = bf16[1,8,2,4,16,2,256]{6,5,4,3,2,1,0:T(2,128)(2,1)S(1)} copy(bf16[1,8,2,4,16,2,256]{6,5,2,4,1,3,0:T(2,128)(2,1)} %bitcast.186) | data formatting | bytes 2097152 | tf_op jit(solution)/shard_map/transpose | solution.py:131
  188.5 2.5 %collective-permute-start.15 = (bf16[1,128,256]{2,1,0:T(8,128)(2,1)S(1)}, bf16[1,128,256]{2,1,0:T(8,128)(2,1)S(1)}, u32[]{:S(2)}, u32[]{:S(2)}) collective-permute-start(bf16[1,128,256]{2,1,0:T(8,128)(2,1)S(1)} %get-tuple-element.49), channel_id=1, source_target_pairs={{0,2},{2,4},{4,6},{6,8},{8,10},{10,12},{12,14},{1,3},{3,5},{5,7},{... | collective-permute-start | bytes 196616 | tf_op jit(solution)/shard_map/ppermute | solution.py:44
  191.1 1.2 reshape_reshape.15
  192.3 3.6 %collective-permute-start.16 = (bf16[1,128,256]{2,1,0:T(8,128)(2,1)S(1)}, bf16[1,128,256]{2,1,0:T(8,128)(2,1)S(1)}, u32[]{:S(2)}, u32[]{:S(2)}) collective-permute-start(bf16[1,128,256]{2,1,0:T(8,128)(2,1)S(1)} %get-tuple-element.48), channel_id=1, source_target_pairs={{2,0},{4,2},{6,4},{8,6},{10,8},{12,10},{14,12},{3,1},{5,3},{7,5},{... | collective-permute-start | bytes 196616 | tf_op jit(solution)/shard_map/ppermute | solution.py:45
  196.0 1.3 collective-permute-done.16
  197.6 1.3 collective-permute-start.17
  198.9 3.5 %collective-permute-start.18 = (bf16[18,1,256]{2,1,0:T(2,128)(2,1)S(1)}, bf16[18,1,256]{2,1,0:T(2,128)(2,1)S(1)}, u32[]{:S(2)}, u32[]{:S(2)}) collective-permute-start(bf16[18,1,256]{2,1,0:T(2,128)(2,1)S(1)} %get-tuple-element.40), channel_id=1, source_target_pairs={{1,0},{3,2},{5,4},{7,6},{9,8},{11,10},{13,12},{15,14},{17,16},{19,... | collective-permute-start | bytes 27656 | tf_op jit(solution)/shard_map/ppermute | solution.py:45
  203.3 3.7 %pad_maximum_fusion.5 = (bf16[16,128,256]{2,1,0:T(8,128)(2,1)S(1)}, bf16[16,128,256]{2,1,0:T(8,128)(2,1)S(1)}, bf16[16,128,256]{2,1,0:T(8,128)(2,1)S(1)}, bf16[1...) fusion(bf16[18,128,256]{2,1,0:T(8,128)(2,1)S(1)} %constant_dynamic-update-slice_, ...), kind=kLoop, calls=%fused_computation.76 | loop fusion | flops 12582912 | bytes 7489536 | tf_op jit(solution)/shard_map/concatenate | solution.py:46
  212.0 4.6 %collective-permute-start.20 = (bf16[1,128,256]{2,1,0:T(8,128)(2,1)S(1)}, bf16[1,128,256]{2,1,0:T(8,128)(2,1)S(1)}, u32[]{:S(2)}, u32[]{:S(2)}) collective-permute-start(bf16[1,128,256]{2,1,0:T(8,128)(2,1)S(1)} %get-tuple-element.44), channel_id=1, source_target_pairs={{2,0},{4,2},{6,4},{8,6},{10,8},{12,10},{14,12},{3,1},{5,3},{7,5},{... | collective-permute-start | bytes 196616 | tf_op jit(solution)/shard_map/ppermute | solution.py:45
  216.6 2.1 collective-permute-start.19
  218.8 3.9 %collective-permute-done.19 = bf16[1,128,256]{2,1,0:T(8,128)(2,1)S(1)} collective-permute-done((bf16[1,128,256]{2,1,0:T(8,128)(2,1)S(1)}, bf16[1,128,256]{2,1,0:T(8,128)(2,1)S(1)}, u32[]{:S(2)}, u32[]{:S(2)}) %collective-permute-start.19) | collective-permute-done | bytes 65568 | tf_op jit(solution)/shard_map/ppermute | solution.py:44
  222.7 1.3 collective-permute-start.21
  224.0 3.8 %collective-permute-start.22 = (bf16[18,1,256]{2,1,0:T(2,128)(2,1)S(1)}, bf16[18,1,256]{2,1,0:T(2,128)(2,1)S(1)}, u32[]{:S(2)}, u32[]{:S(2)}) collective-permute-start(bf16[18,1,256]{2,1,0:T(2,128)(2,1)S(1)} %get-tuple-element.35), channel_id=1, source_target_pairs={{1,0},{3,2},{5,4},{7,6},{9,8},{11,10},{13,12},{15,14},{17,16},{19,... | collective-permute-start | bytes 27656 | tf_op jit(solution)/shard_map/ppermute | solution.py:45
  229.3 1.0 fusion.108
  234.1 1.5 fusion.7
  (80 shorter events, 18.8 us)
Async XLA Ops:
  0.0 147.7 %copy-start = (bf16[1280,1024]{1,0:T(8,128)(2,1)S(1)}, bf16[1280,1024]{1,0:T(8,128)(2,1)}, u32[]{:S(2)}) copy-start(bf16[1280,1024]{1,0:T(8,128)(2,1)} %param.16) | copy-start | bytes 7864324
  3.6 57.8 %all-to-all-start.1 = ((bf16[1,4,128,1280]{3,1,0,2:T(4,128)(2,1)}), bf16[1,4,128,1280]{3,1,0,2:T(4,128)(2,1)}, u32[]{:S(2)}, u32[]{:S(2)}) async-start(bf16[1,4,128,1280]{3,1,0,2:T(4,128)(2,1)} %copy.41), calls=%async_computation.1 | async-start | bytes 2621440 | tf_op jit(solution)/shard_map/all_to_all | solution.py:114
  19.9 1.3 copy-start.4
  36.8 10.2 %collective-permute-start = (bf16[1,1,4,8,1280]{4,3,0,2,1:T(8,128)(2,1)}, bf16[1,1,4,8,1280]{4,3,0,2,1:T(8,128)(2,1)}, u32[]{:S(2)}, u32[]{:S(2)}) collective-permute-start(bf16[1,1,4,8,1280]{4,3,0,2,1:T(8,128)(2,1)} %get-tuple-element.19), channel_id=1, source_target_pairs={{0,1},{1,2},{2,3},{3,4},{4,5},{5,6},{6,7},{7,8},{8,9},{9,10},{10,1... | collective-permute-start | bytes 245768 | tf_op jit(solution)/shard_map/ppermute | solution.py:32
  38.2 11.4 %collective-permute-start.1 = (bf16[1,1,4,8,1280]{4,3,0,2,1:T(8,128)(2,1)}, bf16[1,1,4,8,1280]{4,3,0,2,1:T(8,128)(2,1)}, u32[]{:S(2)}, u32[]{:S(2)}) collective-permute-start(bf16[1,1,4,8,1280]{4,3,0,2,1:T(8,128)(2,1)} %get-tuple-element.18), channel_id=1, source_target_pairs={{0,2},{1,3},{2,4},{3,5},{4,6},{5,7},{6,8},{7,9},{8,10},{9,11},{10,... | collective-permute-start | bytes 245768 | tf_op jit(solution)/shard_map/ppermute | solution.py:32
  39.4 13.0 %collective-permute-start.2 = (bf16[1,1,4,8,1280]{4,3,0,2,1:T(8,128)(2,1)}, bf16[1,1,4,8,1280]{4,3,0,2,1:T(8,128)(2,1)}, u32[]{:S(2)}, u32[]{:S(2)}) collective-permute-start(bf16[1,1,4,8,1280]{4,3,0,2,1:T(8,128)(2,1)} %get-tuple-element.17), channel_id=1, source_target_pairs={{0,3},{1,4},{2,5},{3,6},{4,7},{5,8},{6,9},{7,10},{8,11},{9,12},{10... | collective-permute-start | bytes 245768 | tf_op jit(solution)/shard_map/ppermute | solution.py:32
  39.8 15.0 %collective-permute-start.3 = (bf16[1,1,4,8,1280]{4,3,0,2,1:T(8,128)(2,1)}, bf16[1,1,4,8,1280]{4,3,0,2,1:T(8,128)(2,1)}, u32[]{:S(2)}, u32[]{:S(2)}) collective-permute-start(bf16[1,1,4,8,1280]{4,3,0,2,1:T(8,128)(2,1)} %get-tuple-element.16), channel_id=1, source_target_pairs={{0,4},{1,5},{2,6},{3,7},{4,8},{5,9},{6,10},{7,11},{8,12},{9,13},{1... | collective-permute-start | bytes 245768 | tf_op jit(solution)/shard_map/ppermute | solution.py:32
  41.0 19.2 %collective-permute-start.4 = (bf16[1,1,4,8,1280]{4,3,0,2,1:T(8,128)(2,1)S(1)}, bf16[1,1,4,8,1280]{4,3,0,2,1:T(8,128)(2,1)}, u32[]{:S(2)}, u32[]{:S(2)}) collective-permute-start(bf16[1,1,4,8,1280]{4,3,0,2,1:T(8,128)(2,1)S(1)} %get-tuple-element.15), channel_id=1, source_target_pairs={{0,5},{1,6},{2,7},{3,8},{4,9},{5,10},{6,11},{7,12},{8,13},{9,14},{... | collective-permute-start | bytes 245768 | tf_op jit(solution)/shard_map/ppermute | solution.py:32
  46.9 20.3 %collective-permute-start.5 = (bf16[1,1,4,8,1280]{4,3,0,2,1:T(8,128)(2,1)S(1)}, bf16[1,1,4,8,1280]{4,3,0,2,1:T(8,128)(2,1)}, u32[]{:S(2)}, u32[]{:S(2)}) collective-permute-start(bf16[1,1,4,8,1280]{4,3,0,2,1:T(8,128)(2,1)S(1)} %get-tuple-element.14), channel_id=1, source_target_pairs={{0,6},{1,7},{2,8},{3,9},{4,10},{5,11},{6,12},{7,13},{8,14},{9,15},... | collective-permute-start | bytes 245768 | tf_op jit(solution)/shard_map/ppermute | solution.py:32
  49.6 19.1 %collective-permute-start.6 = (bf16[1,1,4,8,1280]{4,3,0,2,1:T(8,128)(2,1)S(1)}, bf16[1,1,4,8,1280]{4,3,0,2,1:T(8,128)(2,1)}, u32[]{:S(2)}, u32[]{:S(2)}) collective-permute-start(bf16[1,1,4,8,1280]{4,3,0,2,1:T(8,128)(2,1)S(1)} %get-tuple-element.13), channel_id=1, source_target_pairs={{0,7},{1,8},{2,9},{3,10},{4,11},{5,12},{6,13},{7,14},{8,15},{9,0},... | collective-permute-start | bytes 245768 | tf_op jit(solution)/shard_map/ppermute | solution.py:32
  52.4 21.1 %collective-permute-start.7 = (bf16[1,1,4,8,1280]{4,3,0,2,1:T(8,128)(2,1)S(1)}, bf16[1,1,4,8,1280]{4,3,0,2,1:T(8,128)(2,1)}, u32[]{:S(2)}, u32[]{:S(2)}) collective-permute-start(bf16[1,1,4,8,1280]{4,3,0,2,1:T(8,128)(2,1)S(1)} %get-tuple-element.12), channel_id=1, source_target_pairs={{0,8},{1,9},{2,10},{3,11},{4,12},{5,13},{6,14},{7,15},{8,0},{9,1},... | collective-permute-start | bytes 245768 | tf_op jit(solution)/shard_map/ppermute | solution.py:32
  54.8 21.6 %collective-permute-start.8 = (bf16[1,1,4,8,1280]{4,3,0,2,1:T(8,128)(2,1)S(1)}, bf16[1,1,4,8,1280]{4,3,0,2,1:T(8,128)(2,1)}, u32[]{:S(2)}, u32[]{:S(2)}) collective-permute-start(bf16[1,1,4,8,1280]{4,3,0,2,1:T(8,128)(2,1)S(1)} %get-tuple-element.11), channel_id=1, source_target_pairs={{0,9},{1,10},{2,11},{3,12},{4,13},{5,14},{6,15},{7,0},{8,1},{9,2},... | collective-permute-start | bytes 245768 | tf_op jit(solution)/shard_map/ppermute | solution.py:32
  60.2 19.0 %collective-permute-start.9 = (bf16[1,1,4,8,1280]{4,3,0,2,1:T(8,128)(2,1)S(1)}, bf16[1,1,4,8,1280]{4,3,0,2,1:T(8,128)(2,1)S(1)}, u32[]{:S(2)}, u32[]{:S(2)}) collective-permute-start(bf16[1,1,4,8,1280]{4,3,0,2,1:T(8,128)(2,1)S(1)} %get-tuple-element.10), channel_id=1, source_target_pairs={{0,10},{1,11},{2,12},{3,13},{4,14},{5,15},{6,0},{7,1},{8,2},{9,3},... | collective-permute-start | bytes 245768 | tf_op jit(solution)/shard_map/ppermute | solution.py:32
  61.3 58.1 %all-to-all-start = ((bf16[1,4,128,1280]{3,1,0,2:T(4,128)(2,1)}), bf16[1,4,128,1280]{3,1,0,2:T(4,128)(2,1)}, u32[]{:S(2)}, u32[]{:S(2)}) async-start(bf16[1,4,128,1280]{3,1,0,2:T(4,128)(2,1)} %copy.39), calls=%async_computation | async-start | bytes 2621440 | tf_op jit(solution)/shard_map/all_to_all | solution.py:113
  67.2 31.9 %collective-permute-start.10 = (bf16[1,1,4,8,1280]{4,3,0,2,1:T(8,128)(2,1)S(1)}, bf16[1,1,4,8,1280]{4,3,0,2,1:T(8,128)(2,1)S(1)}, u32[]{:S(2)}, u32[]{:S(2)}) collective-permute-start(bf16[1,1,4,8,1280]{4,3,0,2,1:T(8,128)(2,1)S(1)} %get-tuple-element.9), channel_id=1, source_target_pairs={{0,11},{1,12},{2,13},{3,14},{4,15},{5,0},{6,1},{7,2},{8,3},{9,4},{... | collective-permute-start | bytes 245768 | tf_op jit(solution)/shard_map/ppermute | solution.py:32
  68.7 31.2 %collective-permute-start.11 = (bf16[1,1,4,8,1280]{4,3,0,2,1:T(8,128)(2,1)S(1)}, bf16[1,1,4,8,1280]{4,3,0,2,1:T(8,128)(2,1)S(1)}, u32[]{:S(2)}, u32[]{:S(2)}) collective-permute-start(bf16[1,1,4,8,1280]{4,3,0,2,1:T(8,128)(2,1)S(1)} %get-tuple-element.8), channel_id=1, source_target_pairs={{0,12},{1,13},{2,14},{3,15},{4,0},{5,1},{6,2},{7,3},{8,4},{9,5},{1... | collective-permute-start | bytes 245768 | tf_op jit(solution)/shard_map/ppermute | solution.py:32
  73.4 29.1 %collective-permute-start.12 = (bf16[1,1,4,8,1280]{4,3,0,2,1:T(8,128)(2,1)S(1)}, bf16[1,1,4,8,1280]{4,3,0,2,1:T(8,128)(2,1)S(1)}, u32[]{:S(2)}, u32[]{:S(2)}) collective-permute-start(bf16[1,1,4,8,1280]{4,3,0,2,1:T(8,128)(2,1)S(1)} %get-tuple-element.7), channel_id=1, source_target_pairs={{0,13},{1,14},{2,15},{3,0},{4,1},{5,2},{6,3},{7,4},{8,5},{9,6},{10... | collective-permute-start | bytes 245768 | tf_op jit(solution)/shard_map/ppermute | solution.py:32
  76.4 26.8 %collective-permute-start.13 = (bf16[1,1,4,8,1280]{4,3,0,2,1:T(8,128)(2,1)S(1)}, bf16[1,1,4,8,1280]{4,3,0,2,1:T(8,128)(2,1)S(1)}, u32[]{:S(2)}, u32[]{:S(2)}) collective-permute-start(bf16[1,1,4,8,1280]{4,3,0,2,1:T(8,128)(2,1)S(1)} %get-tuple-element.6), channel_id=1, source_target_pairs={{0,14},{1,15},{2,0},{3,1},{4,2},{5,3},{6,4},{7,5},{8,6},{9,7},{10,... | collective-permute-start | bytes 245768 | tf_op jit(solution)/shard_map/ppermute | solution.py:32
  79.1 24.7 %collective-permute-start.14 = (bf16[1,1,4,8,1280]{4,3,0,2,1:T(8,128)(2,1)S(1)}, bf16[1,1,4,8,1280]{4,3,0,2,1:T(8,128)(2,1)S(1)}, u32[]{:S(2)}, u32[]{:S(2)}) collective-permute-start(bf16[1,1,4,8,1280]{4,3,0,2,1:T(8,128)(2,1)S(1)} %get-tuple-element.5), channel_id=1, source_target_pairs={{0,15},{1,0},{2,1},{3,2},{4,3},{5,4},{6,5},{7,6},{8,7},{9,8},{10,9... | collective-permute-start | bytes 245768 | tf_op jit(solution)/shard_map/ppermute | solution.py:32
  131.5 1.3 copy-start.3
  143.1 4.6 %copy-start.9 = (f32[1024]{0:T(1024)S(1)}, f32[1024]{0:T(1024)}, u32[]{:S(2)}) copy-start(f32[1024]{0:T(1024)} %param.17) | copy-start | bytes 12292
  188.5 7.4 %collective-permute-start.15 = (bf16[1,128,256]{2,1,0:T(8,128)(2,1)S(1)}, bf16[1,128,256]{2,1,0:T(8,128)(2,1)S(1)}, u32[]{:S(2)}, u32[]{:S(2)}) collective-permute-start(bf16[1,128,256]{2,1,0:T(8,128)(2,1)S(1)} %get-tuple-element.49), channel_id=1, source_target_pairs={{0,2},{2,4},{4,6},{6,8},{8,10},{10,12},{12,14},{1,3},{3,5},{5,7},{... | collective-permute-start | bytes 196616 | tf_op jit(solution)/shard_map/ppermute | solution.py:44
  192.3 5.0 %collective-permute-start.16 = (bf16[1,128,256]{2,1,0:T(8,128)(2,1)S(1)}, bf16[1,128,256]{2,1,0:T(8,128)(2,1)S(1)}, u32[]{:S(2)}, u32[]{:S(2)}) collective-permute-start(bf16[1,128,256]{2,1,0:T(8,128)(2,1)S(1)} %get-tuple-element.48), channel_id=1, source_target_pairs={{2,0},{4,2},{6,4},{8,6},{10,8},{12,10},{14,12},{3,1},{5,3},{7,5},{... | collective-permute-start | bytes 196616 | tf_op jit(solution)/shard_map/ppermute | solution.py:45
  196.0 6.5 %copy-start.5 = (bf16[3,3,256,256]{3,2,1,0:T(8,128)(2,1)S(1)}, bf16[3,3,256,256]{3,2,1,0:T(8,128)(2,1)}, u32[]{:S(2)}) copy-start(bf16[3,3,256,256]{3,2,1,0:T(8,128)(2,1)} %param.18) | copy-start | bytes 3538948
  197.6 5.7 %collective-permute-start.17 = (bf16[18,1,256]{2,1,0:T(2,128)(2,1)S(1)}, bf16[18,1,256]{2,1,0:T(2,128)(2,1)S(1)}, u32[]{:S(2)}, u32[]{:S(2)}) collective-permute-start(bf16[18,1,256]{2,1,0:T(2,128)(2,1)S(1)} %get-tuple-element.39), channel_id=1, source_target_pairs={{0,1},{2,3},{4,5},{6,7},{8,9},{10,11},{12,13},{14,15},{16,17},{18,... | collective-permute-start | bytes 27656 | tf_op jit(solution)/shard_map/ppermute | solution.py:44
  198.9 4.4 %collective-permute-start.18 = (bf16[18,1,256]{2,1,0:T(2,128)(2,1)S(1)}, bf16[18,1,256]{2,1,0:T(2,128)(2,1)S(1)}, u32[]{:S(2)}, u32[]{:S(2)}) collective-permute-start(bf16[18,1,256]{2,1,0:T(2,128)(2,1)S(1)} %get-tuple-element.40), channel_id=1, source_target_pairs={{1,0},{3,2},{5,4},{7,6},{9,8},{11,10},{13,12},{15,14},{17,16},{19,... | collective-permute-start | bytes 27656 | tf_op jit(solution)/shard_map/ppermute | solution.py:45
  208.4 1.2 copy-start.2
  210.0 0.7 copy-start.7
  212.0 6.7 %collective-permute-start.20 = (bf16[1,128,256]{2,1,0:T(8,128)(2,1)S(1)}, bf16[1,128,256]{2,1,0:T(8,128)(2,1)S(1)}, u32[]{:S(2)}, u32[]{:S(2)}) collective-permute-start(bf16[1,128,256]{2,1,0:T(8,128)(2,1)S(1)} %get-tuple-element.44), channel_id=1, source_target_pairs={{2,0},{4,2},{6,4},{8,6},{10,8},{12,10},{14,12},{3,1},{5,3},{7,5},{... | collective-permute-start | bytes 196616 | tf_op jit(solution)/shard_map/ppermute | solution.py:45
  216.6 11.4 %copy-start.6 = (bf16[3,3,256,256]{3,2,1,0:T(8,128)(2,1)S(1)}, bf16[3,3,256,256]{3,2,1,0:T(8,128)(2,1)}, u32[]{:S(2)}) copy-start(bf16[3,3,256,256]{3,2,1,0:T(8,128)(2,1)} %param.20) | copy-start | bytes 3538948
  216.6 6.0 %collective-permute-start.19 = (bf16[1,128,256]{2,1,0:T(8,128)(2,1)S(1)}, bf16[1,128,256]{2,1,0:T(8,128)(2,1)S(1)}, u32[]{:S(2)}, u32[]{:S(2)}) collective-permute-start(bf16[1,128,256]{2,1,0:T(8,128)(2,1)S(1)} %get-tuple-element.43), channel_id=1, source_target_pairs={{0,2},{2,4},{4,6},{6,8},{8,10},{10,12},{12,14},{1,3},{3,5},{5,7},{... | collective-permute-start | bytes 196616 | tf_op jit(solution)/shard_map/ppermute | solution.py:44
  222.7 5.7 %collective-permute-start.21 = (bf16[18,1,256]{2,1,0:T(2,128)(2,1)S(1)}, bf16[18,1,256]{2,1,0:T(2,128)(2,1)S(1)}, u32[]{:S(2)}, u32[]{:S(2)}) collective-permute-start(bf16[18,1,256]{2,1,0:T(2,128)(2,1)S(1)} %get-tuple-element.34), channel_id=1, source_target_pairs={{0,1},{2,3},{4,5},{6,7},{8,9},{10,11},{12,13},{14,15},{16,17},{18,... | collective-permute-start | bytes 27656 | tf_op jit(solution)/shard_map/ppermute | solution.py:44
  224.0 4.5 %collective-permute-start.22 = (bf16[18,1,256]{2,1,0:T(2,128)(2,1)S(1)}, bf16[18,1,256]{2,1,0:T(2,128)(2,1)S(1)}, u32[]{:S(2)}, u32[]{:S(2)}) collective-permute-start(bf16[18,1,256]{2,1,0:T(2,128)(2,1)S(1)} %get-tuple-element.35), channel_id=1, source_target_pairs={{1,0},{3,2},{5,4},{7,6},{9,8},{11,10},{13,12},{15,14},{17,16},{19,... | collective-permute-start | bytes 27656 | tf_op jit(solution)/shard_map/ppermute | solution.py:45
  233.4 0.7 copy-start.8
  233.9 1.9 copy-start.1
